TPU v7x, 32 devices: a whole 2x2x4 slice. The times are simulated.
32 devices in a mesh: cuts: 16 (over z, x, core), ang: 2 (over y).
Axes of the slice: x: 2, y: 2, z: 4, core: 2. Of those that a mesh axis runs over, the one named last changes fastest.
Arguments:
- projections: bfloat16 [16, 16, 2, 128, 256], P('cuts', None, 'ang'), may hold values from -48 to 48
- start_image: bfloat16 [4096, 1024], P('cuts'), may hold values from 0 to 2
- system: bfloat16 [8, 16, 2, 64, 128], P('ang'), may hold values from 0.0009994507 to 0.029907227
- first_tile: int32 [8, 16], P('ang'), may hold values from 0 to 3, as said below
Outputs:
- new_image: float32 [4096, 1024], P('cuts', 'ang')
- residual: bfloat16 [16, 4096, 256], P('ang', 'cuts')
Inputs may be any that keep to these rules, and one draw needn't show every extreme that they name: In every angle block each bin tile is first_tile of at least one pixel tile; every pixel tile meets exactly two bin tiles, first_tile and first_tile + 1 modulo 4.
All inputs are finite; a program needn't handle non-finite values.
Results may differ from a plain program's by a relative error of at most 0.001.
Values may be sent and summed in bfloat16 or wider, within the bound.
A program may use at most 128 MiB of HBM per device.

v0:
```python
import functools

import jax
import jax.numpy as jnp
from jax import lax
from jax.experimental import pallas as pl
from jax.experimental.pallas import tpu as pltpu
from jax.sharding import PartitionSpec as P

MESH = pl.DeviceIdType.MESH
NT = (((1,), (1,)), ((), ()))
SPLIT = (3, 3, 2)
PUTS = 4
VMEM_BYTES = 67043328 - 0


def kernel(
    C, G, sizes, first_in, proj, image, system, new_out, res_out,
    first, img, sysv, A, F, inv, arr, R, U, own, urecv, colp, crecv,
    first_sem, img_sem, sys_sem, send_sem, arr_sem,
    usend_sem, urecv_sem, csend_sem, crecv_sem,
):
    c = lax.axis_index("cuts")
    a = lax.axis_index("ang")
    T = C // G
    blocks, ptiles, _, W, PW = system.shape
    KR = proj.shape[3]
    NC = len(sizes)
    starts = [sum(sizes[:q]) for q in range(NC)]
    npix = image.shape[1]
    share = npix // G
    bins = proj.shape[4]
    half = bins // PW
    ntiles = bins // W

    tgt = c // T
    slot = a * T + lax.rem(c, T)

    barrier = pltpu.get_barrier_semaphore()
    for i in range(T):
        source = a * T + lax.rem(c + i, T)
        for s in range(1 if i == 0 else 0, G):
            pl.semaphore_signal(
                barrier, inc=1, device_id=(source, lax.rem(a + s, G)), device_id_type=MESH
            )

    @pl.when(tgt != a)
    def _():
        pl.semaphore_signal(
            barrier, inc=1, device_id=(a * T + lax.rem(c, T), a), device_id_type=MESH
        )

    for s in range(1, G):
        pl.semaphore_signal(barrier, inc=1, device_id=(c, lax.rem(a + s, G)), device_id_type=MESH)

    sys_copy = pltpu.make_async_copy(system, sysv, sys_sem)
    sys_copy.start()
    first_copy = pltpu.make_async_copy(first_in, first, first_sem)
    first_copy.start()
    img_copies = []
    for q in range(NC):
        for b in range(G):
            cp = pltpu.make_async_copy(
                image.at[pl.ds(b * KR + starts[q], sizes[q])],
                img.at[pl.ds(G * starts[q] + b * sizes[q], sizes[q])],
                img_sem.at[q, b],
            )
            cp.start()
            img_copies.append(cp)
    pl.semaphore_wait(barrier, C + G - 1 - jnp.where(tgt == a, 1, 0))

    def piece(q, o):
        return pltpu.make_async_remote_copy(
            src_ref=proj.at[0, o, 0, pl.ds(starts[q], sizes[q])],
            dst_ref=arr[q].at[slot],
            send_sem=send_sem,
            recv_sem=arr_sem.at[q],
            device_id=(o, tgt),
            device_id_type=MESH,
        )

    for q in range(NC):
        for s in range(1, C):
            piece(q, lax.rem(c + s, C)).start()

        @pl.when(tgt != a)
        def _(q=q):
            piece(q, c).start()

        @pl.when(tgt == a)
        def _(q=q):
            pltpu.make_async_copy(
                proj.at[0, c, 0, pl.ds(starts[q], sizes[q])], arr[q].at[slot], arr_sem.at[q]
            ).start()

    sys_copy.wait()
    first_copy.wait()


    def build(p, carry):
        rows_p = pl.ds(pl.multiple_of(p * W, W), W)
        for g in range(blocks):
            f = first[g, p]
            w = [sysv[g, p, j].astype(jnp.float32) for j in range(2)]
            r = [pltpu.roll(x, W, 1) for x in w]
            up = (lax.broadcasted_iota(jnp.int32, (W, PW), 1) // W)
            for t in range(PW // W):
                x = [jnp.where(up == t, w[j], r[j]) for j in range(2)]
                for h in range(half):
                    b = up + h * (PW // W)
                    second = lax.rem(f + 1, ntiles)
                    tile = jnp.where(b == f, x[0], jnp.where(b == second, x[1], 0.0))
                    A[g * (PW // W) + t, rows_p, pl.ds(h * PW, PW)] = tile.astype(jnp.bfloat16)
        return carry

    lax.fori_loop(0, ptiles, build, 0)

    colp[...] = jnp.zeros_like(colp)
    for cp in img_copies:
        cp.wait()

    def project(t, carry):
        m = A[t]
        F[t] = jnp.dot(
            img[...], m, preferred_element_type=jnp.float32
        )
        ones_r = jnp.ones((16, npix), jnp.bfloat16)
        ones_b = jnp.ones((16, bins), jnp.bfloat16)
        inv[t] = 1.0 / jnp.dot(ones_r, m, preferred_element_type=jnp.float32)[:8]
        for g in range(G):
            colp[g] += lax.dot_general(
                ones_b, A[t, pl.ds(g * share, share)], NT, preferred_element_type=jnp.float32
            )[:8]
        return carry

    lax.fori_loop(0, T, project, 0)

    for s in range(1, G):
        g = lax.rem(a + s, G)
        pltpu.make_async_remote_copy(
            src_ref=colp.at[g], dst_ref=crecv.at[s - 1], send_sem=csend_sem.at[s - 1],
            recv_sem=crecv_sem, device_id=(c, g), device_id_type=MESH,
        ).start()

    def residual_part(q):
        def body(t, carry):
            scale = inv[t][:1]
            for b in range(G):
                value = arr[q][b * T + t].astype(jnp.float32)
                f = F[t, pl.ds(G * starts[q] + b * sizes[q], sizes[q])]
                res = ((value - f) * scale).astype(jnp.bfloat16)
                R[q][t, pl.ds(b * sizes[q], sizes[q])] = res
                res_out[t, pl.ds(b * KR + starts[q], sizes[q])] = res
            return carry

        lax.fori_loop(0, T, body, 0)

    def back(q, g):
        total = jnp.zeros((G * sizes[q], share), jnp.float32)
        pix = pl.ds(pl.multiple_of(g * share, share), share)
        for t in range(T):
            total = total + lax.dot_general(
                R[q][t], A[t, pix], NT, preferred_element_type=jnp.float32
            )
        return total

    def u_copy(q, s):
        g = lax.rem(a + s, G)
        return pltpu.make_async_remote_copy(
            src_ref=U[q].at[s - 1], dst_ref=urecv[q].at[s - 1],
            send_sem=usend_sem.at[q, s - 1], recv_sem=urecv_sem.at[q, s - 1],
            device_id=(c, g), device_id_type=MESH,
        )

    def process(q):
        pltpu.make_async_copy(arr[q], arr[q], arr_sem.at[q]).wait()
        residual_part(q)
        for s in range(1, G):
            U[q][s - 1] = back(q, lax.rem(a + s, G))
            u_copy(q, s).start()
        own[q][...] = back(q, a)

    def finish(q):
        total = own[q][...]
        for s in range(1, G):
            u_copy(q, s).wait_recv()
            total = total + urecv[q][s - 1]
        mine = img[
            pl.ds(G * starts[q], G * sizes[q]), pl.ds(pl.multiple_of(a * share, share), share)
        ]
        new = mine.astype(jnp.float32) + total * own_inv
        for b in range(G):
            new_out[pl.ds(b * KR + starts[q], sizes[q])] = new[b * sizes[q] : (b + 1) * sizes[q]]

    pltpu.make_async_copy(crecv, crecv, crecv_sem).wait()
    columns = colp[a][:1]
    for s in range(1, G):
        columns = columns + crecv[s - 1][:1]
    own_inv = 1.0 / columns
    for q in range(NC):
        process(q)
        if q >= 1:
            finish(q - 1)
    finish(NC - 1)

    @pl.when(tgt == a)
    def _():
        sent = proj.at[0, pl.ds(0, C - 1)]
        pltpu.make_async_copy(sent, sent, send_sem).wait()

    @pl.when(tgt != a)
    def _():
        pltpu.make_async_copy(proj.at[0], proj.at[0], send_sem).wait()

    for s in range(1, G):
        pltpu.make_async_remote_copy(
            src_ref=colp.at[0], dst_ref=crecv.at[s - 1], send_sem=csend_sem.at[s - 1],
            recv_sem=crecv_sem, device_id=(c, lax.rem(a + s, G)), device_id_type=MESH,
        ).wait_send()
    for q in range(NC):
        for s in range(1, G):
            u_copy(q, s).wait_send()


def put_out(new_in, res_in, new_out, res_out, sem):
    copies = []
    for i, (src, dst) in enumerate(((new_in, new_out), (res_in, res_out))):
        n = src.shape[0] // PUTS
        for k in range(PUTS):
            part = pl.ds(k * n, n)
            copies.append(pltpu.make_async_copy(src.at[part], dst.at[part], sem.at[i * PUTS + k]))
    for cp in copies:
        cp.start()
    for cp in copies:
        cp.wait()


def chunk_sizes(rows):
    unit = max(16, rows // sum(SPLIT))
    sizes = [n * unit for n in SPLIT]
    if sum(sizes) == rows:
        return sizes
    return [16] * (rows // 16) if rows % 16 == 0 else [rows]


def on_device(C, G, projections, start_image, system, first_tile):
    T = C // G
    KR = projections.shape[3]
    sizes = chunk_sizes(KR)
    NC = len(sizes)
    slices, npix = start_image.shape
    bins = projections.shape[4]
    share = npix // G
    bf16, f32 = jnp.bfloat16, jnp.float32
    dma = pltpu.SemaphoreType.DMA
    out_bytes = slices * share * 4 + T * slices * bins * 2
    new_image, residual = pl.pallas_call(
        functools.partial(kernel, C, G, sizes),
        out_shape=(
            pltpu.VMEM((slices, share), f32),
            pltpu.VMEM((T, slices, bins), bf16),
        ),
        in_specs=[pl.BlockSpec(memory_space=pltpu.HBM)] * 4,
        out_specs=(pl.BlockSpec(memory_space=pltpu.VMEM),) * 2,
        scratch_shapes=[
            pltpu.SMEM(first_tile.shape, jnp.int32),
            pltpu.VMEM((slices, npix), bf16),
            pltpu.VMEM(system.shape, bf16),
            pltpu.VMEM((T, npix, bins), bf16),
            pltpu.VMEM((T, slices, bins), f32),
            pltpu.VMEM((T, 8, bins), f32),
            [pltpu.VMEM((C, n, bins), bf16) for n in sizes],
            [pltpu.VMEM((T, G * n, bins), bf16) for n in sizes],
            [pltpu.VMEM((G - 1, G * n, share), f32) for n in sizes],
            [pltpu.VMEM((G * n, share), f32) for n in sizes],
            [pltpu.VMEM((G - 1, G * n, share), f32) for n in sizes],
            pltpu.VMEM((G, 8, share), f32),
            pltpu.VMEM((G - 1, 8, share), f32),
            dma,
            dma((NC, G)),
            dma,
            dma,
            dma((NC,)),
            dma((NC, G - 1)),
            dma((NC, G - 1)),
            dma((G - 1,)),
            dma,
        ],
        compiler_params=pltpu.CompilerParams(
            collective_id=0, has_side_effects=True, vmem_limit_bytes=VMEM_BYTES - out_bytes
        ),
    )(first_tile, projections, start_image, system)
    return pl.pallas_call(
        put_out,
        out_shape=(
            jax.ShapeDtypeStruct(new_image.shape, f32),
            jax.ShapeDtypeStruct(residual.shape, bf16),
        ),
        in_specs=[pl.BlockSpec(memory_space=pl.ANY)] * 2,
        out_specs=(pl.BlockSpec(memory_space=pl.ANY),) * 2,
        scratch_shapes=[dma((2 * PUTS,))],
        compiler_params=pltpu.CompilerParams(vmem_limit_bytes=1 << 20),
    )(new_image, residual)


def solution(mesh):
    in_specs = (
        P("cuts", None, "ang", None, None),
        P("cuts", None),
        P("ang", None, None, None, None),
        P("ang", None),
    )
    out_specs = (P("cuts", "ang"), P("ang", "cuts", None))
    return jax.shard_map(
        functools.partial(on_device, mesh.shape["cuts"], mesh.shape["ang"]),
        mesh=mesh, in_specs=in_specs, out_specs=out_specs, check_vma=False,
    )
```

profile of v0, /device:TPU:10, one launch (start us, length us, event | category | flops | bytes accessed | tf_op | source)
XLA Modules:
  0.0 38.4 jit_solution(6036984188709287909)
XLA Ops:
  0.6 36.5 %shard_map.59 = (f32[256,512]{1,0:T(8,128)S(1)}, bf16[8,256,256]{2,1,0:T(8,128)(2,1)S(1)}) custom-call(s32[4,16]{1,0:T(4,128)} %first_in.1, bf16[1,16,1,128,256]{4,3,2,1,0:T(8,128)(2,1)} %proj.1, bf16[256,1024]{1,0:T(8,128)(2,1)} %image.1, bf16[4,16,2,64,128]{4,3,2,1,0:T(8,128)(2,1)} %system.1), custom_call_target="tpu_custom_call" | custom-call | tf_op jit(solution)/shard_map/pallas_call | solution.py:257
  37.1 1.2 %shard_map.60 = (f32[256,512]{1,0:T(8,128)}, bf16[8,256,256]{2,1,0:T(8,128)(2,1)}) custom-call(f32[256,512]{1,0:T(8,128)S(1)} %get-tuple-element.4.new_in, bf16[8,256,256]{2,1,0:T(8,128)(2,1)S(1)} %get-tuple-element.5.res_in), custom_call_target="tpu_custom_call" | custom-call | tf_op jit(solution)/shard_map/pallas_call | solution.py:293
where the time goes:
time: 38.5 us; the launch traced here: 38.4 us
  Pallas kernels  37.7 us (98%)
  between operations  0.64 us (2%)
    pallas_call x1, Pallas kernels, on_device(): pl.pallas_call(functools.partial(kernel, C, G, sizes), out_shape=(pltpu.V...  36.5 us
    pallas_call x1, Pallas kernels, on_device(): pl.pallas_call(put_out, out_shape=(jax.ShapeDtypeStruct(new_image.shape,...  1.21 us

commit v1 on v0

v1 whole, which is shorter than its diff:
```python
import functools

import jax
import jax.numpy as jnp
from jax import lax
from jax.experimental import pallas as pl
from jax.experimental.pallas import tpu as pltpu
from jax.sharding import PartitionSpec as P

MESH = pl.DeviceIdType.MESH
NT = (((1,), (1,)), ((), ()))
SPLIT = (3, 2, 1, 1, 1)
TURN = (0, 1, 2, 2, 2)
LATE = 3
PUTS = 2
PAD = 16
VMEM_BYTES = 67043328


def kernel(
    C, G, sizes, first_in, proj, image, system, new_out, res_out,
    first, img, sysv, A, F, R, arr, U, own, urecv, colp, crecv,
    first_sem, img_sem, sys_sem, send_sem, arr_sem, go_sem,
    usend_sem, urecv_sem, csend_sem, crecv_sem,
):
    c = lax.axis_index("cuts")
    a = lax.axis_index("ang")
    T = C // G
    blocks, ptiles, _, W, PW = system.shape
    KR = proj.shape[3]
    NC = len(sizes)
    starts = [sum(sizes[:q]) for q in range(NC)]
    slices, npix = image.shape
    share = npix // G
    bins = proj.shape[4]
    ntiles = bins // W
    pair = PW // W

    tgt = c // T
    slot = a * T + lax.rem(c, T)

    barrier = pltpu.get_barrier_semaphore()
    for i in range(T):
        source = a * T + lax.rem(c + i, T)
        for s in range(1 if i == 0 else 0, G):
            pl.semaphore_signal(
                barrier, inc=1, device_id=(source, lax.rem(a + s, G)), device_id_type=MESH
            )

    @pl.when(tgt != a)
    def _():
        pl.semaphore_signal(
            barrier, inc=1, device_id=(a * T + lax.rem(c, T), a), device_id_type=MESH
        )

    for s in range(1, G):
        pl.semaphore_signal(barrier, inc=1, device_id=(c, lax.rem(a + s, G)), device_id_type=MESH)

    def flip(m):
        o = c
        for b in range(C.bit_length() - 1):
            if (m >> b) & 1:
                o = o + (1 - 2 * lax.rem(c // (1 << b), 2)) * (1 << b)
        return o

    paced = G == 2 and C & (C - 1) == 0 and T > 1
    mate = flip(T // 2) if paced else c
    if paced:
        @pl.when(tgt != a)
        def _():
            pl.semaphore_signal(barrier, inc=1, device_id=(mate, a), device_id_type=MESH)

    sys_copy = pltpu.make_async_copy(system, sysv, sys_sem)
    sys_copy.start()
    first_copy = pltpu.make_async_copy(first_in, first, first_sem)
    first_copy.start()
    img_copies = []
    for q in range(NC):
        for b in range(G):
            cp = pltpu.make_async_copy(
                image.at[pl.ds(b * KR + starts[q], sizes[q])],
                img.at[pl.ds(G * starts[q] + b * sizes[q], sizes[q])],
                img_sem.at[q, b],
            )
            cp.start()
            img_copies.append(cp)
    away = jnp.where(tgt == a, 0, 1)
    pl.semaphore_wait(barrier, C + G - 2 + (2 * away if paced else away))

    def piece(q, o):
        return pltpu.make_async_remote_copy(
            src_ref=proj.at[0, o, 0, pl.ds(starts[q], sizes[q])],
            dst_ref=arr[q].at[slot],
            send_sem=send_sem.at[q],
            recv_sem=arr_sem.at[q],
            device_id=(o, tgt),
            device_id_type=MESH,
        )

    turn = TURN[:NC] if paced and NC == len(TURN) else (0,) * NC
    turns = max(turn) + 1
    inner = tgt + lax.rem(c, T) // max(T // 2, 1) == 1
    order = [flip(m) for m in range(C - 1, 0, -1)] if paced else [lax.rem(c + s, C) for s in range(1, C)]
    AHEAD = 2 if paced else 0

    def send_ahead(q):
        if AHEAD and q < NC:
            @pl.when(tgt == G - 1)
            def _():
                for o in range(AHEAD):
                    piece(q, o).start()

    def send_rest(q):
        for o in order:
            if AHEAD:
                @pl.when((tgt != G - 1) | (o >= AHEAD))
                def _(o=o):
                    piece(q, o).start()
            else:
                piece(q, o).start()

        @pl.when(tgt != a)
        def _():
            piece(q, c).start()

        @pl.when(tgt == a)
        def _():
            pltpu.make_async_copy(
                proj.at[0, c, 0, pl.ds(starts[q], sizes[q])], arr[q].at[slot], arr_sem.at[q]
            ).start()

    def send(q):
        send_ahead(q + 1)
        send_rest(q)

    def sent(q):
        rows = pl.ds(starts[q], sizes[q])

        @pl.when(tgt == a)
        def _():
            part = proj.at[0, pl.ds(0, C - 1), 0, rows]
            pltpu.make_async_copy(part, part, send_sem.at[q]).wait()

        @pl.when(tgt != a)
        def _():
            part = proj.at[0, :, 0, rows]
            pltpu.make_async_copy(part, part, send_sem.at[q]).wait()

    def of_turn(k):
        return [q for q in range(NC) if turn[q] == k]

    send_ahead(0)
    for q in of_turn(0):
        send(q)
    if turns > 1:
        @pl.when(inner)
        def _():
            for k in range(1, turns):
                for q in of_turn(k):
                    send(q)

    def take_turn(k):
        if k >= turns:
            return

        @pl.when(inner)
        def _():
            for q in of_turn(k - 1):
                sent(q)
            pl.semaphore_signal(go_sem.at[k - 1], inc=1, device_id=(mate, a), device_id_type=MESH)

        @pl.when(jnp.logical_not(inner))
        def _():
            pl.semaphore_wait(go_sem.at[k - 1], 1)
            for q in of_turn(k):
                send(q)

    img[pl.ds(slices, PAD)] = jnp.ones((PAD, npix), jnp.bfloat16)
    R[pl.ds(0, PAD)] = jnp.ones((PAD, T * bins), jnp.bfloat16)
    sys_copy.wait()
    first_copy.wait()

    def build(i, carry):
        lane = lax.broadcasted_iota(jnp.int32, (W, pair * W), 1) // W
        cols = pl.ds(pl.multiple_of(i * pair * W, pair * W), pair * W)
        for g in range(blocks):
            x = [
                jnp.concatenate([sysv[g, i * pair + k, j] for k in range(pair)], axis=0)
                .astype(jnp.float32).T.astype(jnp.bfloat16)
                for j in range(2)
            ]
            f = jnp.full(lane.shape, first[g, i * pair], jnp.int32)
            for k in range(1, pair):
                f = jnp.where(lane == k, first[g, i * pair + k], f)
            second = jnp.where(f == ntiles - 1, 0, f + 1)
            for b in range(ntiles):
                m0, m1 = f == b, second == b
                for t in range(pair):
                    part = slice(t * W, (t + 1) * W)
                    tile = jnp.where(m0, x[0][part], jnp.where(m1, x[1][part], jnp.zeros((), jnp.bfloat16)))
                    A[pl.ds((g * pair + t) * bins + b * W, W), cols] = tile
        return carry

    lax.fori_loop(0, ptiles // pair, build, 0)

    for cp in img_copies:
        cp.wait()

    def project(t, carry):
        m = A[pl.ds(pl.multiple_of(t * bins, bins), bins)]
        F[t] = lax.dot_general(img[...], m, NT, preferred_element_type=jnp.float32)
        return carry

    lax.fori_loop(0, T, project, 0)

    def residual_part(q):
        def body(t, carry):
            scale = 1.0 / F[t, pl.ds(slices, 8)][:1]
            for b in range(G):
                value = arr[q][b * T + t].astype(jnp.float32)
                f = F[t, pl.ds(G * starts[q] + b * sizes[q], sizes[q])]
                res = ((value - f) * scale).astype(jnp.bfloat16)
                R[
                    pl.ds(PAD + G * starts[q] + b * sizes[q], sizes[q]),
                    pl.ds(pl.multiple_of(t * bins, bins), bins),
                ] = res
                res_out[t, pl.ds(b * KR + starts[q], sizes[q])] = res
            return carry

        lax.fori_loop(0, T, body, 0)

    def back(lo, hi, g):
        return jnp.dot(
            R[pl.ds(lo, hi - lo)],
            A[:, pl.ds(pl.multiple_of(g * share, share), share)],
            preferred_element_type=jnp.float32,
        )

    def col_copy(s):
        g = lax.rem(a + s, G)
        return pltpu.make_async_remote_copy(
            src_ref=colp.at[g], dst_ref=crecv.at[s - 1], send_sem=csend_sem.at[s - 1],
            recv_sem=crecv_sem, device_id=(c, g), device_id_type=MESH,
        )

    def u_copy(q, s):
        g = lax.rem(a + s, G)
        return pltpu.make_async_remote_copy(
            src_ref=U[q].at[s - 1], dst_ref=urecv[q].at[s - 1],
            send_sem=usend_sem.at[q, s - 1], recv_sem=urecv_sem.at[q, s - 1],
            device_id=(c, g), device_id_type=MESH,
        )

    def own_back(lo, hi):
        y = back(lo, hi, a)
        if lo == 0:
            colp[a] = y[:8]
            y = y[PAD:]
            lo = PAD
        own[pl.ds(lo - PAD, hi - lo)] = y

    def process(q):
        pltpu.make_async_copy(arr[q], arr[q], arr_sem.at[q]).wait()
        residual_part(q)
        lo = 0 if q == 0 else PAD + G * starts[q]
        hi = PAD + G * (starts[q] + sizes[q])
        for s in range(1, G):
            y = back(lo, hi, lax.rem(a + s, G))
            if q == 0:
                colp[lax.rem(a + s, G)] = y[:8]
                y = y[PAD:]
            U[q][s - 1] = y
            u_copy(q, s).start()
            if q == 0:
                col_copy(s).start()
        late = max(NC - LATE, 0)
        if q < late:
            own_back(lo, hi)
        elif q == NC - 1:
            own_back(0 if late == 0 else PAD + G * starts[late], hi)

    def finish(q, own_inv):
        total = own[pl.ds(G * starts[q], G * sizes[q])]
        for s in range(1, G):
            u_copy(q, s).wait_recv()
            total = total + urecv[q][s - 1]
        mine = img[
            pl.ds(G * starts[q], G * sizes[q]), pl.ds(pl.multiple_of(a * share, share), share)
        ]
        new = mine.astype(jnp.float32) + total * own_inv
        for b in range(G):
            new_out[pl.ds(b * KR + starts[q], sizes[q])] = new[b * sizes[q] : (b + 1) * sizes[q]]

    take_turn(1)
    for q in range(NC):
        process(q)
        take_turn(q + 2)

    pltpu.make_async_copy(crecv, crecv, crecv_sem).wait()
    columns = colp[a][:1]
    for s in range(1, G):
        columns = columns + crecv[s - 1][:1]
    own_inv = 1.0 / columns
    for q in range(NC):
        finish(q, own_inv)

    for q in range(NC):
        if turn[q] == turns - 1:
            sent(q)
        else:
            @pl.when(jnp.logical_not(inner))
            def _(q=q):
                sent(q)

    for s in range(1, G):
        col_copy(s).wait_send()
    for q in range(NC):
        for s in range(1, G):
            u_copy(q, s).wait_send()


def put_out(new_in, res_in, new_out, res_out, sem):
    copies = []
    for i, (src, dst) in enumerate(((new_in, new_out), (res_in, res_out))):
        n = src.shape[0] // PUTS
        for k in range(PUTS):
            part = pl.ds(k * n, n)
            copies.append(pltpu.make_async_copy(src.at[part], dst.at[part], sem.at[i * PUTS + k]))
    for cp in copies:
        cp.start()
    for cp in copies:
        cp.wait()


def chunk_sizes(rows):
    unit = max(16, rows // sum(SPLIT))
    sizes = [n * unit for n in SPLIT]
    if sum(sizes) == rows:
        return sizes
    return [16] * (rows // 16) if rows % 16 == 0 else [rows]


def on_device(C, G, projections, start_image, system, first_tile):
    T = C // G
    KR = projections.shape[3]
    sizes = chunk_sizes(KR)
    NC = len(sizes)
    slices, npix = start_image.shape
    bins = projections.shape[4]
    share = npix // G
    bf16, f32 = jnp.bfloat16, jnp.float32
    dma = pltpu.SemaphoreType.DMA
    out_bytes = slices * share * 4 + T * slices * bins * 2
    new_image, residual = pl.pallas_call(
        functools.partial(kernel, C, G, sizes),
        out_shape=(
            pltpu.VMEM((slices, share), f32),
            pltpu.VMEM((T, slices, bins), bf16),
        ),
        in_specs=[pl.BlockSpec(memory_space=pltpu.HBM)] * 4,
        out_specs=(pl.BlockSpec(memory_space=pltpu.VMEM),) * 2,
        scratch_shapes=[
            pltpu.SMEM(first_tile.shape, jnp.int32),
            pltpu.VMEM((slices + PAD, npix), bf16),
            pltpu.VMEM(system.shape, bf16),
            pltpu.VMEM((T * bins, npix), bf16),
            pltpu.VMEM((T, slices + PAD, bins), f32),
            pltpu.VMEM((slices + PAD, T * bins), bf16),
            [pltpu.VMEM((C, n, bins), bf16) for n in sizes],
            [pltpu.VMEM((G - 1, G * n, share), f32) for n in sizes],
            pltpu.VMEM((slices, share), f32),
            [pltpu.VMEM((G - 1, G * n, share), f32) for n in sizes],
            pltpu.VMEM((G, 8, share), f32),
            pltpu.VMEM((G - 1, 8, share), f32),
            dma,
            dma((NC, G)),
            dma,
            dma((NC,)),
            dma((NC,)),
            pltpu.SemaphoreType.REGULAR((max(NC, 2),)),
            dma((NC, G - 1)),
            dma((NC, G - 1)),
            dma((G - 1,)),
            dma,
        ],
        compiler_params=pltpu.CompilerParams(
            collective_id=0, has_side_effects=True, vmem_limit_bytes=VMEM_BYTES - out_bytes
        ),
    )(first_tile, projections, start_image, system)
    return pl.pallas_call(
        put_out,
        out_shape=(
            jax.ShapeDtypeStruct(new_image.shape, f32),
            jax.ShapeDtypeStruct(residual.shape, bf16),
        ),
        in_specs=[pl.BlockSpec(memory_space=pl.ANY)] * 2,
        out_specs=(pl.BlockSpec(memory_space=pl.ANY),) * 2,
        scratch_shapes=[dma((2 * PUTS,))],
        compiler_params=pltpu.CompilerParams(vmem_limit_bytes=1 << 20),
    )(new_image, residual)


def solution(mesh):
    in_specs = (
        P("cuts", None, "ang", None, None),
        P("cuts", None),
        P("ang", None, None, None, None),
        P("ang", None),
    )
    out_specs = (P("cuts", "ang"), P("ang", "cuts", None))
    return jax.shard_map(
        functools.partial(on_device, mesh.shape["cuts"], mesh.shape["ang"]),
        mesh=mesh, in_specs=in_specs, out_specs=out_specs, check_vma=False,
    )
```

time: 38.5 us -> 37.5 us (0.974)
  the two profiles are of different devices: /device:TPU:10 before, /device:TPU:2 now
where the time goes in v1:
time: 37.5 us; the launch traced here: 37.1 us
  Pallas kernels  36.5 us (97%)
  between operations  0.64 us (2%)
    pallas_call x1, Pallas kernels, on_device(): pl.pallas_call(functools.partial(kernel, C, G, sizes), out_shape=(pltpu.V...  35.3 us
    pallas_call x1, Pallas kernels, on_device(): pl.pallas_call(put_out, out_shape=(jax.ShapeDtypeStruct(new_image.shape,...  1.18 us

profile of v1, /device:TPU:2, one launch (start us, length us, event | category | flops | bytes accessed | tf_op | source)
XLA Modules:
  0.0 37.1 jit_solution(12912528883805578485)
XLA Ops:
  0.6 35.3 %shard_map.59 = (f32[256,512]{1,0:T(8,128)S(1)}, bf16[8,256,256]{2,1,0:T(8,128)(2,1)S(1)}) custom-call(s32[4,16]{1,0:T(4,128)} %first_in.1, bf16[1,16,1,128,256]{4,3,2,1,0:T(8,128)(2,1)} %proj.1, bf16[256,1024]{1,0:T(8,128)(2,1)} %image.1, bf16[4,16,2,64,128]{4,3,2,1,0:T(8,128)(2,1)} %system.1), custom_call_target="tpu_custom_call" | custom-call | tf_op jit(solution)/shard_map/pallas_call | solution.py:354
  35.9 1.2 %shard_map.60 = (f32[256,512]{1,0:T(8,128)}, bf16[8,256,256]{2,1,0:T(8,128)(2,1)}) custom-call(f32[256,512]{1,0:T(8,128)S(1)} %get-tuple-element.4.new_in, bf16[8,256,256]{2,1,0:T(8,128)(2,1)S(1)} %get-tuple-element.5.res_in), custom_call_target="tpu_custom_call" | custom-call | tf_op jit(solution)/shard_map/pallas_call | solution.py:390

commit v2 on v1

--- a/solution.py
+++ b/solution.py
@@ -14,14 +14,16 @@
 LATE = 3
 PUTS = 2
 PAD = 16
+STEPS = 32767.0
+TINY = 1e-30
 VMEM_BYTES = 67043328
 
 
 def kernel(
     C, G, sizes, first_in, proj, image, system, new_out, res_out,
-    first, img, sysv, A, F, R, arr, U, own, urecv, colp, crecv,
+    first, img, sysv, A, F, R, arr, U, unit, own, urecv, unitrecv, colp, crecv,
     first_sem, img_sem, sys_sem, send_sem, arr_sem, go_sem,
-    usend_sem, urecv_sem, csend_sem, crecv_sem,
+    usend_sem, urecv_sem, nsend_sem, nrecv_sem, csend_sem, crecv_sem,
 ):
     c = lax.axis_index("cuts")
     a = lax.axis_index("ang")
@@ -251,6 +253,14 @@
             device_id=(c, g), device_id_type=MESH,
         )
 
+    def unit_copy(q, s):
+        g = lax.rem(a + s, G)
+        return pltpu.make_async_remote_copy(
+            src_ref=unit[q].at[s - 1], dst_ref=unitrecv[q].at[s - 1],
+            send_sem=nsend_sem.at[q, s - 1], recv_sem=nrecv_sem.at[q, s - 1],
+            device_id=(c, g), device_id_type=MESH,
+        )
+
     def own_back(lo, hi):
         y = back(lo, hi, a)
         if lo == 0:
@@ -269,7 +279,10 @@
             if q == 0:
                 colp[lax.rem(a + s, G)] = y[:8]
                 y = y[PAD:]
-            U[q][s - 1] = y
+            top = jnp.maximum(jnp.max(jnp.abs(y), axis=0, keepdims=True), TINY)
+            unit[q][s - 1] = top * (1.0 / STEPS)
+            U[q][s - 1] = jnp.round(y * (STEPS / top)).astype(jnp.int32).astype(jnp.int16)
+            unit_copy(q, s).start()
             u_copy(q, s).start()
             if q == 0:
                 col_copy(s).start()
@@ -283,7 +296,8 @@
         total = own[pl.ds(G * starts[q], G * sizes[q])]
         for s in range(1, G):
             u_copy(q, s).wait_recv()
-            total = total + urecv[q][s - 1]
+            unit_copy(q, s).wait_recv()
+            total = total + urecv[q][s - 1].astype(jnp.int32).astype(jnp.float32) * unitrecv[q][s - 1]
         mine = img[
             pl.ds(G * starts[q], G * sizes[q]), pl.ds(pl.multiple_of(a * share, share), share)
         ]
@@ -317,6 +331,7 @@
     for q in range(NC):
         for s in range(1, G):
             u_copy(q, s).wait_send()
+            unit_copy(q, s).wait_send()
 
 
 def put_out(new_in, res_in, new_out, res_out, sem):
@@ -367,9 +382,11 @@
             pltpu.VMEM((T, slices + PAD, bins), f32),
             pltpu.VMEM((slices + PAD, T * bins), bf16),
             [pltpu.VMEM((C, n, bins), bf16) for n in sizes],
-            [pltpu.VMEM((G - 1, G * n, share), f32) for n in sizes],
+            [pltpu.VMEM((G - 1, G * n, share), jnp.int16) for n in sizes],
+            [pltpu.VMEM((G - 1, 1, share), f32) for n in sizes],
             pltpu.VMEM((slices, share), f32),
-            [pltpu.VMEM((G - 1, G * n, share), f32) for n in sizes],
+            [pltpu.VMEM((G - 1, G * n, share), jnp.int16) for n in sizes],
+            [pltpu.VMEM((G - 1, 1, share), f32) for n in sizes],
             pltpu.VMEM((G, 8, share), f32),
             pltpu.VMEM((G - 1, 8, share), f32),
             dma,
@@ -378,6 +395,8 @@
             dma((NC,)),
             dma((NC,)),
             pltpu.SemaphoreType.REGULAR((max(NC, 2),)),
+            dma((NC, G - 1)),
+            dma((NC, G - 1)),
             dma((NC, G - 1)),
             dma((NC, G - 1)),
             dma((G - 1,)),

time: 37.5 us -> 36.6 us (0.976)
  Pallas kernels: 36.5 us -> 35.8 us
    pallas_call x1, Pallas kernels: 35.3 us -> 34.6 us  [on_device(): pl.pallas_call(functools.partial(kernel, C, G, sizes), out_shape=(pltpu.V...]
where the time goes in v2:
time: 36.6 us; the launch traced here: 36.4 us
  Pallas kernels  35.8 us (98%)
  between operations  0.64 us (2%)
    pallas_call x1, Pallas kernels, on_device(): pl.pallas_call(functools.partial(kernel, C, G, sizes), out_shape=(pltpu.V...  34.6 us
    pallas_call x1, Pallas kernels, on_device(): pl.pallas_call(put_out, out_shape=(jax.ShapeDtypeStruct(new_image.shape,...  1.18 us

profile of v2, /device:TPU:2, one launch (start us, length us, event | category | flops | bytes accessed | tf_op | source)
XLA Modules:
  0.0 36.4 jit_solution(16041723850194243898)
XLA Ops:
  0.6 34.6 %shard_map.59 = (f32[256,512]{1,0:T(8,128)S(1)}, bf16[8,256,256]{2,1,0:T(8,128)(2,1)S(1)}) custom-call(s32[4,16]{1,0:T(4,128)} %first_in.1, bf16[1,16,1,128,256]{4,3,2,1,0:T(8,128)(2,1)} %proj.1, bf16[256,1024]{1,0:T(8,128)(2,1)} %image.1, bf16[4,16,2,64,128]{4,3,2,1,0:T(8,128)(2,1)} %system.1), custom_call_target="tpu_custom_call" | custom-call | tf_op jit(solution)/shard_map/pallas_call | solution.py:369
  35.2 1.2 %shard_map.60 = (f32[256,512]{1,0:T(8,128)}, bf16[8,256,256]{2,1,0:T(8,128)(2,1)}) custom-call(f32[256,512]{1,0:T(8,128)S(1)} %get-tuple-element.4.new_in, bf16[8,256,256]{2,1,0:T(8,128)(2,1)S(1)} %get-tuple-element.5.res_in), custom_call_target="tpu_custom_call" | custom-call | tf_op jit(solution)/shard_map/pallas_call | solution.py:409

commit v3 on v2

--- a/solution.py
+++ b/solution.py
@@ -22,7 +22,7 @@
 def kernel(
     C, G, sizes, first_in, proj, image, system, new_out, res_out,
     first, img, sysv, A, F, R, arr, U, unit, own, urecv, unitrecv, colp, crecv,
-    first_sem, img_sem, sys_sem, send_sem, arr_sem, go_sem,
+    first_sem, img_sem, sys_sem, send_sem, arr_sem, go_sem, up_sem,
     usend_sem, urecv_sem, nsend_sem, nrecv_sem, csend_sem, crecv_sem,
 ):
     c = lax.axis_index("cuts")
@@ -41,23 +41,6 @@
     tgt = c // T
     slot = a * T + lax.rem(c, T)
 
-    barrier = pltpu.get_barrier_semaphore()
-    for i in range(T):
-        source = a * T + lax.rem(c + i, T)
-        for s in range(1 if i == 0 else 0, G):
-            pl.semaphore_signal(
-                barrier, inc=1, device_id=(source, lax.rem(a + s, G)), device_id_type=MESH
-            )
-
-    @pl.when(tgt != a)
-    def _():
-        pl.semaphore_signal(
-            barrier, inc=1, device_id=(a * T + lax.rem(c, T), a), device_id_type=MESH
-        )
-
-    for s in range(1, G):
-        pl.semaphore_signal(barrier, inc=1, device_id=(c, lax.rem(a + s, G)), device_id_type=MESH)
-
     def flip(m):
         o = c
         for b in range(C.bit_length() - 1):
@@ -66,11 +49,41 @@
         return o
 
     paced = G == 2 and C & (C - 1) == 0 and T > 1
-    mate = flip(T // 2) if paced else c
+    half = T // 2
+    inner = tgt + lax.rem(c, T) // max(half, 1) == 1
+    outer = jnp.logical_not(inner)
+    mate = flip(half) if paced else c
+    barrier = pltpu.get_barrier_semaphore()
+
+    def greet(device, where=barrier):
+        pl.semaphore_signal(where, inc=1, device_id=device, device_id_type=MESH)
+
     if paced:
         @pl.when(tgt != a)
         def _():
-            pl.semaphore_signal(barrier, inc=1, device_id=(mate, a), device_id_type=MESH)
+            for m in range(T, C):
+                for s in range(G):
+                    greet((flip(m), s))
+
+        for m in range(half):
+            for s in range(1 if m == 0 else 0, G):
+                greet((flip(m), lax.rem(a + s, G)))
+
+        @pl.when(inner)
+        def _():
+            greet((mate, a))
+    else:
+        for i in range(T):
+            source = a * T + lax.rem(c + i, T)
+            for s in range(1 if i == 0 else 0, G):
+                greet((source, lax.rem(a + s, G)))
+
+        @pl.when(tgt != a)
+        def _():
+            greet((a * T + lax.rem(c, T), a))
+
+        for s in range(1, G):
+            greet((c, lax.rem(a + s, G)))
 
     sys_copy = pltpu.make_async_copy(system, sysv, sys_sem)
     sys_copy.start()
@@ -86,14 +99,16 @@
             )
             cp.start()
             img_copies.append(cp)
-    away = jnp.where(tgt == a, 0, 1)
-    pl.semaphore_wait(barrier, C + G - 2 + (2 * away if paced else away))
-
-    def piece(q, o):
+    if paced:
+        pl.semaphore_wait(barrier, C - T + G * half - 1 + jnp.where(inner, 0, 1))
+    else:
+        pl.semaphore_wait(barrier, C + G - 2 + jnp.where(tgt == a, 0, 1))
+
+    def piece(q, o, k=0):
         return pltpu.make_async_remote_copy(
             src_ref=proj.at[0, o, 0, pl.ds(starts[q], sizes[q])],
             dst_ref=arr[q].at[slot],
-            send_sem=send_sem.at[q],
+            send_sem=send_sem.at[q, k],
             recv_sem=arr_sem.at[q],
             device_id=(o, tgt),
             device_id_type=MESH,
@@ -101,9 +116,28 @@
 
     turn = TURN[:NC] if paced and NC == len(TURN) else (0,) * NC
     turns = max(turn) + 1
-    inner = tgt + lax.rem(c, T) // max(T // 2, 1) == 1
-    order = [flip(m) for m in range(C - 1, 0, -1)] if paced else [lax.rem(c + s, C) for s in range(1, C)]
     AHEAD = 2 if paced else 0
+
+    def send_self(q, k):
+        @pl.when(tgt != a)
+        def _():
+            piece(q, c, k).start()
+
+        @pl.when(tgt == a)
+        def _():
+            pltpu.make_async_copy(
+                proj.at[0, c, 0, pl.ds(starts[q], sizes[q])], arr[q].at[slot], arr_sem.at[q]
+            ).start()
+
+    def send_plane(q):
+        for m in range(half - 1, 0, -1):
+            piece(q, flip(m), 1).start()
+        send_self(q, 1)
+
+    def send_half():
+        for q in range(NC):
+            for m in range(T - 1, half - 1, -1):
+                piece(q, flip(m), 1).start()
 
     def send_ahead(q):
         if AHEAD and q < NC:
@@ -112,54 +146,55 @@
                 for o in range(AHEAD):
                     piece(q, o).start()
 
-    def send_rest(q):
-        for o in order:
-            if AHEAD:
-                @pl.when((tgt != G - 1) | (o >= AHEAD))
-                def _(o=o):
-                    piece(q, o).start()
-            else:
-                piece(q, o).start()
-
-        @pl.when(tgt != a)
-        def _():
-            piece(q, c).start()
-
-        @pl.when(tgt == a)
-        def _():
-            pltpu.make_async_copy(
-                proj.at[0, c, 0, pl.ds(starts[q], sizes[q])], arr[q].at[slot], arr_sem.at[q]
-            ).start()
-
     def send(q):
         send_ahead(q + 1)
-        send_rest(q)
+        for m in range(T, C):
+            o = flip(m)
+
+            @pl.when((tgt != G - 1) | (o >= AHEAD))
+            def _(o=o):
+                piece(q, o).start()
+
+    def sent_blocks(q, k, n):
+        part = proj.at[0, pl.ds(0, n), 0, pl.ds(starts[q], sizes[q])]
+        pltpu.make_async_copy(part, part, send_sem.at[q, k]).wait()
 
     def sent(q):
-        rows = pl.ds(starts[q], sizes[q])
-
-        @pl.when(tgt == a)
-        def _():
-            part = proj.at[0, pl.ds(0, C - 1), 0, rows]
-            pltpu.make_async_copy(part, part, send_sem.at[q]).wait()
-
-        @pl.when(tgt != a)
-        def _():
-            part = proj.at[0, :, 0, rows]
-            pltpu.make_async_copy(part, part, send_sem.at[q]).wait()
+        sent_blocks(q, 0, C - T)
 
     def of_turn(k):
         return [q for q in range(NC) if turn[q] == k]
 
-    send_ahead(0)
-    for q in of_turn(0):
-        send(q)
-    if turns > 1:
+    if paced:
+        send_ahead(0)
+        for q in of_turn(0):
+            send(q)
+        if turns > 1:
+            @pl.when(inner)
+            def _():
+                for k in range(1, turns):
+                    for q in of_turn(k):
+                        send(q)
+        for q in range(NC):
+            send_plane(q)
+
+        @pl.when(outer)
+        def _():
+            greet((mate, a), up_sem)
+    else:
+        for q in range(NC):
+            for i in range(1, C):
+                piece(q, lax.rem(c + i, C)).start()
+            send_self(q, 0)
+
+    def meet():
+        pl.semaphore_wait(up_sem, 1)
+
         @pl.when(inner)
         def _():
-            for k in range(1, turns):
-                for q in of_turn(k):
-                    send(q)
+            greet((mate, a), up_sem)
+
+        send_half()
 
     def take_turn(k):
         if k >= turns:
@@ -171,7 +206,7 @@
                 sent(q)
             pl.semaphore_signal(go_sem.at[k - 1], inc=1, device_id=(mate, a), device_id_type=MESH)
 
-        @pl.when(jnp.logical_not(inner))
+        @pl.when(outer)
         def _():
             pl.semaphore_wait(go_sem.at[k - 1], 1)
             for q in of_turn(k):
@@ -204,6 +239,8 @@
         return carry
 
     lax.fori_loop(0, ptiles // pair, build, 0)
+    if paced:
+        meet()
 
     for cp in img_copies:
         cp.wait()
@@ -319,12 +356,30 @@
         finish(q, own_inv)
 
     for q in range(NC):
+        if not paced:
+            @pl.when(tgt == a)
+            def _(q=q):
+                sent_blocks(q, 0, C - 1)
+
+            @pl.when(tgt != a)
+            def _(q=q):
+                sent_blocks(q, 0, C)
+
+            continue
         if turn[q] == turns - 1:
             sent(q)
         else:
-            @pl.when(jnp.logical_not(inner))
+            @pl.when(outer)
             def _(q=q):
                 sent(q)
+
+        @pl.when(tgt == a)
+        def _(q=q):
+            sent_blocks(q, 1, T - 1)
+
+        @pl.when(tgt != a)
+        def _(q=q):
+            sent_blocks(q, 1, T)
 
     for s in range(1, G):
         col_copy(s).wait_send()
@@ -392,9 +447,10 @@
             dma,
             dma((NC, G)),
             dma,
-            dma((NC,)),
+            dma((NC, 2)),
             dma((NC,)),
             pltpu.SemaphoreType.REGULAR((max(NC, 2),)),
+            pltpu.SemaphoreType.REGULAR,
             dma((NC, G - 1)),
             dma((NC, G - 1)),
             dma((NC, G - 1)),

time: 36.6 us -> 35.5 us (0.970)
  Pallas kernels: 35.8 us -> 34.6 us
    pallas_call x1, Pallas kernels: 34.6 us -> 33.4 us  [on_device(): pl.pallas_call(functools.partial(kernel, C, G, sizes), out_shape=(pltpu.V...]
where the time goes in v3:
time: 35.5 us; the launch traced here: 35.2 us
  Pallas kernels  34.6 us (97%)
  between operations  0.64 us (2%)
    pallas_call x1, Pallas kernels, on_device(): pl.pallas_call(functools.partial(kernel, C, G, sizes), out_shape=(pltpu.V...  33.4 us
    pallas_call x1, Pallas kernels, on_device(): pl.pallas_call(put_out, out_shape=(jax.ShapeDtypeStruct(new_image.shape,...  1.18 us

profile of v3, /device:TPU:2, one launch (start us, length us, event | category | flops | bytes accessed | tf_op | source)
XLA Modules:
  0.0 35.2 jit_solution(15349681866968701895)
XLA Ops:
  0.6 33.4 %shard_map.59 = (f32[256,512]{1,0:T(8,128)S(1)}, bf16[8,256,256]{2,1,0:T(8,128)(2,1)S(1)}) custom-call(s32[4,16]{1,0:T(4,128)} %first_in.1, bf16[1,16,1,128,256]{4,3,2,1,0:T(8,128)(2,1)} %proj.1, bf16[256,1024]{1,0:T(8,128)(2,1)} %image.1, bf16[4,16,2,64,128]{4,3,2,1,0:T(8,128)(2,1)} %system.1), custom_call_target="tpu_custom_call" | custom-call | tf_op jit(solution)/shard_map/pallas_call | solution.py:424
  34.0 1.2 %shard_map.60 = (f32[256,512]{1,0:T(8,128)}, bf16[8,256,256]{2,1,0:T(8,128)(2,1)}) custom-call(f32[256,512]{1,0:T(8,128)S(1)} %get-tuple-element.4.new_in, bf16[8,256,256]{2,1,0:T(8,128)(2,1)S(1)} %get-tuple-element.5.res_in), custom_call_target="tpu_custom_call" | custom-call | tf_op jit(solution)/shard_map/pallas_call | solution.py:465

commit v4 on v3

--- a/solution.py
+++ b/solution.py
@@ -9,9 +9,9 @@
 
 MESH = pl.DeviceIdType.MESH
 NT = (((1,), (1,)), ((), ()))
-SPLIT = (3, 2, 1, 1, 1)
-TURN = (0, 1, 2, 2, 2)
-LATE = 3
+SPLIT = (2, 2, 2, 2)
+TURN = (0, 1, 2, 2)
+LATE = 2
 PUTS = 2
 PAD = 16
 STEPS = 32767.0
@@ -117,6 +117,7 @@
     turn = TURN[:NC] if paced and NC == len(TURN) else (0,) * NC
     turns = max(turn) + 1
     AHEAD = 2 if paced else 0
+    CROSS = sorted(range(T, C), key=lambda m: (m & half, -(m & (half // 2)), m))
 
     def send_self(q, k):
         @pl.when(tgt != a)
@@ -148,7 +149,7 @@
 
     def send(q):
         send_ahead(q + 1)
-        for m in range(T, C):
+        for m in CROSS:
             o = flip(m)
 
             @pl.when((tgt != G - 1) | (o >= AHEAD))
@@ -352,7 +353,7 @@
     for s in range(1, G):
         columns = columns + crecv[s - 1][:1]
     own_inv = 1.0 / columns
-    for q in range(NC):
+    for q in range(NC - 1):
         finish(q, own_inv)
 
     for q in range(NC):
@@ -384,6 +385,8 @@
     for s in range(1, G):
         col_copy(s).wait_send()
     for q in range(NC):
+        if q == NC - 1:
+            finish(q, own_inv)
         for s in range(1, G):
             u_copy(q, s).wait_send()
             unit_copy(q, s).wait_send()

time: 35.5 us -> 34.6 us (0.975)
  Pallas kernels: 34.6 us -> 33.7 us
    pallas_call x1, Pallas kernels: 33.4 us -> 32.6 us  [on_device(): pl.pallas_call(functools.partial(kernel, C, G, sizes), out_shape=(pltpu.V...]
where the time goes in v4:
time: 34.6 us; the launch traced here: 34.4 us
  Pallas kernels  33.7 us (97%)
  between operations  0.64 us (2%)
    pallas_call x1, Pallas kernels, on_device(): pl.pallas_call(functools.partial(kernel, C, G, sizes), out_shape=(pltpu.V...  32.6 us
    pallas_call x1, Pallas kernels, on_device(): pl.pallas_call(put_out, out_shape=(jax.ShapeDtypeStruct(new_image.shape,...  1.18 us

profile of v4, /device:TPU:2, one launch (start us, length us, event | category | flops | bytes accessed | tf_op | source)
XLA Modules:
  0.0 34.4 jit_solution(12490307692625025429)
XLA Ops:
  0.6 32.6 %shard_map.59 = (f32[256,512]{1,0:T(8,128)S(1)}, bf16[8,256,256]{2,1,0:T(8,128)(2,1)S(1)}) custom-call(s32[4,16]{1,0:T(4,128)} %first_in.1, bf16[1,16,1,128,256]{4,3,2,1,0:T(8,128)(2,1)} %proj.1, bf16[256,1024]{1,0:T(8,128)(2,1)} %image.1, bf16[4,16,2,64,128]{4,3,2,1,0:T(8,128)(2,1)} %system.1), custom_call_target="tpu_custom_call" | custom-call | tf_op jit(solution)/shard_map/pallas_call | solution.py:427
  33.2 1.2 %shard_map.60 = (f32[256,512]{1,0:T(8,128)}, bf16[8,256,256]{2,1,0:T(8,128)(2,1)}) custom-call(f32[256,512]{1,0:T(8,128)S(1)} %get-tuple-element.4.new_in, bf16[8,256,256]{2,1,0:T(8,128)(2,1)S(1)} %get-tuple-element.5.res_in), custom_call_target="tpu_custom_call" | custom-call | tf_op jit(solution)/shard_map/pallas_call | solution.py:468

commit v5 on v4

--- a/solution.py
+++ b/solution.py
@@ -16,13 +16,14 @@
 PAD = 16
 STEPS = 32767.0
 TINY = 1e-30
+ROUND = 12582912.0
 VMEM_BYTES = 67043328
 
 
 def kernel(
     C, G, sizes, first_in, proj, image, system, new_out, res_out,
-    first, img, sysv, A, F, R, arr, U, unit, own, urecv, unitrecv, colp, crecv,
-    first_sem, img_sem, sys_sem, send_sem, arr_sem, go_sem, up_sem,
+    held, first, img, sysv, A, F, R, arr, U, unit, own, urecv, unitrecv, colp, crecv,
+    held_sem, first_sem, img_sem, sys_sem, send_sem, arr_sem, go_sem, up_sem,
     usend_sem, urecv_sem, nsend_sem, nrecv_sem, csend_sem, crecv_sem,
 ):
     c = lax.axis_index("cuts")
@@ -49,6 +50,8 @@
         return o
 
     paced = G == 2 and C & (C - 1) == 0 and T > 1
+    held_copy = pltpu.make_async_copy(proj.at[0, :, 0], held, held_sem)
+    held_copy.start()
     half = T // 2
     inner = tgt + lax.rem(c, T) // max(half, 1) == 1
     outer = jnp.logical_not(inner)
@@ -104,9 +107,11 @@
     else:
         pl.semaphore_wait(barrier, C + G - 2 + jnp.where(tgt == a, 0, 1))
 
+    held_copy.wait()
+
     def piece(q, o, k=0):
         return pltpu.make_async_remote_copy(
-            src_ref=proj.at[0, o, 0, pl.ds(starts[q], sizes[q])],
+            src_ref=held.at[o, pl.ds(starts[q], sizes[q])],
             dst_ref=arr[q].at[slot],
             send_sem=send_sem.at[q, k],
             recv_sem=arr_sem.at[q],
@@ -127,7 +132,7 @@
         @pl.when(tgt == a)
         def _():
             pltpu.make_async_copy(
-                proj.at[0, c, 0, pl.ds(starts[q], sizes[q])], arr[q].at[slot], arr_sem.at[q]
+                held.at[c, pl.ds(starts[q], sizes[q])], arr[q].at[slot], arr_sem.at[q]
             ).start()
 
     def send_plane(q):
@@ -157,7 +162,7 @@
                 piece(q, o).start()
 
     def sent_blocks(q, k, n):
-        part = proj.at[0, pl.ds(0, n), 0, pl.ds(starts[q], sizes[q])]
+        part = held.at[pl.ds(0, n), pl.ds(starts[q], sizes[q])]
         pltpu.make_async_copy(part, part, send_sem.at[q, k]).wait()
 
     def sent(q):
@@ -319,7 +324,7 @@
                 y = y[PAD:]
             top = jnp.maximum(jnp.max(jnp.abs(y), axis=0, keepdims=True), TINY)
             unit[q][s - 1] = top * (1.0 / STEPS)
-            U[q][s - 1] = jnp.round(y * (STEPS / top)).astype(jnp.int32).astype(jnp.int16)
+            U[q][s - 1] = ((y * (STEPS / top) + ROUND) - ROUND).astype(jnp.int32).astype(jnp.int16)
             unit_copy(q, s).start()
             u_copy(q, s).start()
             if q == 0:
@@ -330,16 +335,17 @@
         elif q == NC - 1:
             own_back(0 if late == 0 else PAD + G * starts[late], hi)
 
+    def prepare(own_inv):
+        mine = img[pl.ds(0, slices), pl.ds(pl.multiple_of(a * share, share), share)]
+        own[...] = mine.astype(jnp.float32) + own[...] * own_inv
+
     def finish(q, own_inv):
-        total = own[pl.ds(G * starts[q], G * sizes[q])]
+        new = own[pl.ds(G * starts[q], G * sizes[q])]
         for s in range(1, G):
+            unit_copy(q, s).wait_recv()
+            scale = unitrecv[q][s - 1] * own_inv
             u_copy(q, s).wait_recv()
-            unit_copy(q, s).wait_recv()
-            total = total + urecv[q][s - 1].astype(jnp.int32).astype(jnp.float32) * unitrecv[q][s - 1]
-        mine = img[
-            pl.ds(G * starts[q], G * sizes[q]), pl.ds(pl.multiple_of(a * share, share), share)
-        ]
-        new = mine.astype(jnp.float32) + total * own_inv
+            new = new + urecv[q][s - 1].astype(jnp.int32).astype(jnp.float32) * scale
         for b in range(G):
             new_out[pl.ds(b * KR + starts[q], sizes[q])] = new[b * sizes[q] : (b + 1) * sizes[q]]
 
@@ -353,6 +359,7 @@
     for s in range(1, G):
         columns = columns + crecv[s - 1][:1]
     own_inv = 1.0 / columns
+    prepare(own_inv)
     for q in range(NC - 1):
         finish(q, own_inv)
 
@@ -433,6 +440,7 @@
         in_specs=[pl.BlockSpec(memory_space=pltpu.HBM)] * 4,
         out_specs=(pl.BlockSpec(memory_space=pltpu.VMEM),) * 2,
         scratch_shapes=[
+            pltpu.VMEM((C, KR, bins), bf16),
             pltpu.SMEM(first_tile.shape, jnp.int32),
             pltpu.VMEM((slices + PAD, npix), bf16),
             pltpu.VMEM(system.shape, bf16),
@@ -447,6 +455,7 @@
             [pltpu.VMEM((G - 1, 1, share), f32) for n in sizes],
             pltpu.VMEM((G, 8, share), f32),
             pltpu.VMEM((G - 1, 8, share), f32),
+            dma,
             dma,
             dma((NC, G)),
             dma,

time: 34.6 us -> 34.4 us (level)
  no operation moved by 1% of the time
where the time goes in v5:
time: 34.4 us; the launch traced here: 34.2 us
  Pallas kernels  33.5 us (97%)
  between operations  0.64 us (2%)
    pallas_call x1, Pallas kernels, on_device(): pl.pallas_call(functools.partial(kernel, C, G, sizes), out_shape=(pltpu.V...  32.4 us
    pallas_call x1, Pallas kernels, on_device(): pl.pallas_call(put_out, out_shape=(jax.ShapeDtypeStruct(new_image.shape,...  1.18 us

profile of v5, /device:TPU:2, one launch (start us, length us, event | category | flops | bytes accessed | tf_op | source)
XLA Modules:
  0.0 34.2 jit_solution(9121478847018767390)
XLA Ops:
  0.6 32.4 %shard_map.59 = (f32[256,512]{1,0:T(8,128)S(1)}, bf16[8,256,256]{2,1,0:T(8,128)(2,1)S(1)}) custom-call(s32[4,16]{1,0:T(4,128)} %first_in.1, bf16[1,16,1,128,256]{4,3,2,1,0:T(8,128)(2,1)} %proj.1, bf16[256,1024]{1,0:T(8,128)(2,1)} %image.1, bf16[4,16,2,64,128]{4,3,2,1,0:T(8,128)(2,1)} %system.1), custom_call_target="tpu_custom_call" | custom-call | tf_op jit(solution)/shard_map/pallas_call | solution.py:434
  33.0 1.2 %shard_map.60 = (f32[256,512]{1,0:T(8,128)}, bf16[8,256,256]{2,1,0:T(8,128)(2,1)}) custom-call(f32[256,512]{1,0:T(8,128)S(1)} %get-tuple-element.4.new_in, bf16[8,256,256]{2,1,0:T(8,128)(2,1)S(1)} %get-tuple-element.5.res_in), custom_call_target="tpu_custom_call" | custom-call | tf_op jit(solution)/shard_map/pallas_call | solution.py:477

commit v6 on v5

--- a/solution.py
+++ b/solution.py
@@ -10,7 +10,7 @@
 MESH = pl.DeviceIdType.MESH
 NT = (((1,), (1,)), ((), ()))
 SPLIT = (2, 2, 2, 2)
-TURN = (0, 1, 2, 2)
+TURN = (0, 1, 1, 1)
 LATE = 2
 PUTS = 2
 PAD = 16

time: 34.4 us -> 34.4 us (level)
  no operation moved by 1% of the time
where the time goes in v6:
time: 34.4 us; the launch traced here: 34.2 us
  Pallas kernels  33.5 us (97%)
  between operations  0.64 us (2%)
    pallas_call x1, Pallas kernels, on_device(): pl.pallas_call(functools.partial(kernel, C, G, sizes), out_shape=(pltpu.V...  32.4 us
    pallas_call x1, Pallas kernels, on_device(): pl.pallas_call(put_out, out_shape=(jax.ShapeDtypeStruct(new_image.shape,...  1.18 us

profile of v6, /device:TPU:2, one launch (start us, length us, event | category | flops | bytes accessed | tf_op | source)
XLA Modules:
  0.0 34.2 jit_solution(6864482324261158668)
XLA Ops:
  0.6 32.4 %shard_map.59 = (f32[256,512]{1,0:T(8,128)S(1)}, bf16[8,256,256]{2,1,0:T(8,128)(2,1)S(1)}) custom-call(s32[4,16]{1,0:T(4,128)} %first_in.1, bf16[1,16,1,128,256]{4,3,2,1,0:T(8,128)(2,1)} %proj.1, bf16[256,1024]{1,0:T(8,128)(2,1)} %image.1, bf16[4,16,2,64,128]{4,3,2,1,0:T(8,128)(2,1)} %system.1), custom_call_target="tpu_custom_call" | custom-call | tf_op jit(solution)/shard_map/pallas_call | solution.py:434
  33.0 1.2 %shard_map.60 = (f32[256,512]{1,0:T(8,128)}, bf16[8,256,256]{2,1,0:T(8,128)(2,1)}) custom-call(f32[256,512]{1,0:T(8,128)S(1)} %get-tuple-element.4.new_in, bf16[8,256,256]{2,1,0:T(8,128)(2,1)S(1)} %get-tuple-element.5.res_in), custom_call_target="tpu_custom_call" | custom-call | tf_op jit(solution)/shard_map/pallas_call | solution.py:477

commit v7 on v5

--- a/solution.py
+++ b/solution.py
@@ -12,7 +12,7 @@
 SPLIT = (2, 2, 2, 2)
 TURN = (0, 1, 2, 2)
 LATE = 2
-PUTS = 2
+PUTS = 1
 PAD = 16
 STEPS = 32767.0
 TINY = 1e-30

time: 34.4 us -> 34.4 us (level)
  no operation moved by 1% of the time
where the time goes in v7:
time: 34.4 us; the launch traced here: 34.2 us
  Pallas kernels  33.5 us (97%)
  between operations  0.64 us (2%)
    pallas_call x1, Pallas kernels, on_device(): pl.pallas_call(functools.partial(kernel, C, G, sizes), out_shape=(pltpu.V...  32.4 us
    pallas_call x1, Pallas kernels, on_device(): pl.pallas_call(put_out, out_shape=(jax.ShapeDtypeStruct(new_image.shape,...  1.16 us

profile of v7, /device:TPU:2, one launch (start us, length us, event | category | flops | bytes accessed | tf_op | source)
XLA Modules:
  0.0 34.2 jit_solution(16537702663782414812)
XLA Ops:
  0.6 32.4 %shard_map.59 = (f32[256,512]{1,0:T(8,128)S(1)}, bf16[8,256,256]{2,1,0:T(8,128)(2,1)S(1)}) custom-call(s32[4,16]{1,0:T(4,128)} %first_in.1, bf16[1,16,1,128,256]{4,3,2,1,0:T(8,128)(2,1)} %proj.1, bf16[256,1024]{1,0:T(8,128)(2,1)} %image.1, bf16[4,16,2,64,128]{4,3,2,1,0:T(8,128)(2,1)} %system.1), custom_call_target="tpu_custom_call" | custom-call | tf_op jit(solution)/shard_map/pallas_call | solution.py:434
  33.0 1.2 %shard_map.60 = (f32[256,512]{1,0:T(8,128)}, bf16[8,256,256]{2,1,0:T(8,128)(2,1)}) custom-call(f32[256,512]{1,0:T(8,128)S(1)} %get-tuple-element.4.new_in, bf16[8,256,256]{2,1,0:T(8,128)(2,1)S(1)} %get-tuple-element.5.res_in), custom_call_target="tpu_custom_call" | custom-call | tf_op jit(solution)/shard_map/pallas_call | solution.py:477
